TPU v7x, 128 devices: a whole 4x4x4 slice. The times are simulated.
128 devices in a mesh: rep: 4 (over y), wide: 32 (over x, z, core).
Axes of the slice: x: 4, y: 4, z: 4, core: 2. Of those that a mesh axis runs over, the one named last changes fastest.
Arguments:
- hot_table: bfloat16 [65536, 128], P('wide'), may hold values from -3 to 3
- cold_table: bfloat16 [262144, 128], P(('rep', 'wide')), may hold values from -3 to 3
- bag_of: int32 [128, 6144], P(('rep', 'wide')), may hold values from 0 to 4095, never falling along the last dimension, each value on 1 to 4 neighbouring positions
- owner: int32 [786432, 1], P(('rep', 'wide')), may hold values from 0 to 159; in each aligned block of 6144 rows (0 to 6143, 6144 to 12287, ...) at most 64 rows name the same one
- row_in: int32 [786432], P(('rep', 'wide')), may hold values from 0 to 2047
- cross_down: bfloat16 [4096, 256], replicated, may hold values from -0.09375 to 0.09375
- cross_up: bfloat16 [4096, 256], replicated, may hold values from -0.375 to 0.375
- cross_bias: float32 [4096], replicated, may hold values from -3 to 3
- top_weight: bfloat16 [4096, 512], replicated, may hold values from -0.09375 to 0.09375
- d_hidden: bfloat16 [16384, 512], P(('rep', 'wide')), may hold values from -6 to 6
Outputs:
- grad_up: float32 [4096, 256], P(('rep', 'wide'))
- grad_down: float32 [4096, 256], P(('rep', 'wide'))
- grad_top: float32 [4096, 512], P(('rep', 'wide'))
- hot_grad: float32 [65536, 128], P('wide')
- cold_grad: float32 [262144, 128], P(('rep', 'wide'))
Inputs may be any that keep to these rules, and one draw needn't show every extreme that they name: Destination of each lookup: below 32 the holder of hot rows at that wide index in the asking device's own rep group, else the holder of cold rows numbered owner minus 32 over rep+wide. Among the 6144 lookups of one device no destination is named more than 64 times, and in every draw some device names some destination exactly 64 times. `bag_of`: never falls along one device's lookups; each of a device's 4096 bags has 1 to 4 lookups, and some bag has 4. Bag b is sample b // 32, feature b % 32 of the device.
All inputs are finite; a program needn't handle non-finite values.
Results may differ from a plain program's by a relative error of at most 0.0064.
Values may be sent and summed in bfloat16 or wider, within the bound.
A program may use at most 128 MiB of HBM per device.

v0:
```python
import math

import jax
import jax.numpy as jnp
from jax import lax
from jax.sharding import PartitionSpec as P


def in_blocks(value, dim, devices):
    dims = value.shape
    blocks = value.reshape(*dims[:dim], devices, dims[dim] // devices, *dims[dim + 1 :])
    return jnp.moveaxis(blocks, dim, 0)


def summed_on_arrival(value, axis, dim):
    blocks = in_blocks(value, dim, lax.axis_size(axis))
    arrived = lax.all_to_all(blocks, axis, split_axis=0, concat_axis=0, tiled=True)
    return arrived.sum(axis=0)


def sent_to_all(value, axis):
    copies = jnp.broadcast_to(value, (lax.axis_size(axis), *value.shape))
    return lax.all_to_all(copies, axis, split_axis=0, concat_axis=0, tiled=True)


def of_everyone(value, axis):
    everything = sent_to_all(value, axis)
    return jnp.sum(everything, axis=0)


def blocked(total, values, fn):
    block = math.gcd(total, 512)
    index_blocks = jnp.arange(total, dtype=jnp.int32).reshape(total // block, block)
    if values is None:
        result = lax.map(fn, index_blocks)
    else:
        result = lax.map(
            lambda pair: fn(pair[0], pair[1]), (index_blocks, values.reshape(total // block, block))
        )
    return jax.tree.map(lambda part: part.reshape((total,) + part.shape[2:]), result)


def accumulate(incoming, asked, rows_dev, width):
    capacity = asked.shape[-1]
    sources = asked.size // capacity
    group = 1
    for cand in range(1, sources + 1):
        if sources % cand == 0 and cand * capacity <= 2048:
            group = cand
    steps_count = sources // group
    inc_blocks = incoming.reshape(steps_count, group * capacity, width)
    ask_blocks = asked.reshape(steps_count, group * capacity)
    row_ids = jnp.arange(rows_dev, dtype=jnp.int32)

    def add_block(total, pair):
        inc_block, ask_block = pair
        selector = (row_ids[:, None] == ask_block[None, :]).astype(jnp.bfloat16)
        return (total + jnp.dot(selector, inc_block, preferred_element_type=jnp.float32), None)

    summed, unused = lax.scan(
        add_block, jnp.zeros((rows_dev, width), jnp.float32), (inc_blocks, ask_blocks)
    )
    return summed


def body(
    hot_table,
    cold_table,
    bag_of,
    owner,
    row_in,
    cross_down,
    cross_up,
    cross_bias,
    top_weight,
    d_hidden,
):
    n_rep = lax.axis_size("rep")
    n_wide = lax.axis_size("wide")
    shards = n_rep * n_wide
    dests = n_wide + shards
    look_dev = row_in.shape[0]
    rows_dev = hot_table.shape[0]
    width = hot_table.shape[1]
    batch_dev = d_hidden.shape[0]
    feat_width = cross_down.shape[0]
    rank_width = cross_down.shape[1]
    top_units = top_weight.shape[1]
    features = feat_width // width
    bags_dev = batch_dev * features
    grad_cols = 2 * rank_width + top_units
    capacity = max(8, (3 * look_dev // (2 * dests) + 7) // 8 * 8)
    bag_list = bag_of[0]
    dest_list = owner[:, 0]
    positions = jnp.arange(look_dev, dtype=jnp.int32)

    def rank_block(ids, dest_block):
        earlier = (dest_list[None, :] == dest_block[:, None]) & (positions[None, :] < ids[:, None])
        return jnp.sum(earlier.astype(jnp.int32), axis=1)

    ranks = blocked(look_dev, dest_list, rank_block)
    slots = dest_list * capacity + ranks
    slot_total = dests * capacity

    def slot_info_block(ids):
        match = slots[None, :] == ids[:, None]
        used = jnp.sum(match.astype(jnp.int32), axis=1)
        row_pick = jnp.sum(jnp.where(match, row_in[None, :], 0), axis=1)
        bag_pick = jnp.sum(jnp.where(match, bag_list[None, :], 0), axis=1)
        return (used, row_pick, bag_pick)

    used_count, row_pick, bag_pick = blocked(slot_total, None, slot_info_block)
    filled = used_count > 0
    request = jnp.where(filled, row_pick, rows_dev)
    hot_request = request[: n_wide * capacity].reshape(n_wide, capacity)
    cold_request = request[n_wide * capacity :]
    pieces = lax.all_to_all(hot_request, "wide", split_axis=0, concat_axis=0, tiled=True)
    found = jnp.take(hot_table, pieces, axis=0, mode="fill", fill_value=0)
    hot_back = lax.all_to_all(found, "wide", split_axis=0, concat_axis=0, tiled=True)
    hot_asked = pieces
    pieces = lax.all_to_all(
        cold_request.reshape(shards, capacity),
        ("rep", "wide"),
        split_axis=0,
        concat_axis=0,
        tiled=True,
    )
    found = jnp.take(cold_table, pieces, axis=0, mode="fill", fill_value=0)
    cold_back = lax.all_to_all(found, ("rep", "wide"), split_axis=0, concat_axis=0, tiled=True)
    returned = jnp.concatenate([hot_back.reshape(-1, width), cold_back.reshape(-1, width)], axis=0)
    look_rows = returned[slots]
    bag_block = math.gcd(bags_dev, 512)
    bag_starts = jnp.arange(bags_dev // bag_block, dtype=jnp.int32) * bag_block
    bag_offsets = jnp.arange(bag_block, dtype=jnp.int32)

    def pool_block(first):
        selector = ((first + bag_offsets)[:, None] == bag_list[None, :]).astype(jnp.bfloat16)
        return jnp.dot(selector, look_rows, preferred_element_type=jnp.float32)

    pooled = lax.map(pool_block, bag_starts)
    base = pooled.reshape(batch_dev, feat_width).astype(jnp.bfloat16)
    low = jnp.dot(base, cross_down, preferred_element_type=jnp.float32).astype(jnp.bfloat16)
    cross = (
        lax.dot_general(low, cross_up, (((1,), (1,)), ((), ())), preferred_element_type=jnp.float32)
        + cross_bias
    )
    base_full = base.astype(jnp.float32)
    mixed = (base_full * cross + base_full).astype(jnp.bfloat16)
    preact = jnp.dot(mixed, top_weight, preferred_element_type=jnp.float32)
    sigm = jax.nn.sigmoid(preact)
    d_pre = (d_hidden.astype(jnp.float32) * sigm * (1.0 + preact * (1.0 - sigm))).astype(
        jnp.bfloat16
    )
    d_mixed = lax.dot_general(
        d_pre, top_weight, (((1,), (1,)), ((), ())), preferred_element_type=jnp.float32
    )
    d_cross = (d_mixed * base_full).astype(jnp.bfloat16)
    d_low = jnp.dot(d_cross, cross_up, preferred_element_type=jnp.float32).astype(jnp.bfloat16)
    d_base = (
        d_mixed * (cross + 1.0)
        + lax.dot_general(
            d_low, cross_down, (((1,), (1,)), ((), ())), preferred_element_type=jnp.float32
        )
    ).astype(jnp.bfloat16)
    scale_factor = 1.0 / math.sqrt(batch_dev * shards)
    share = feat_width // shards
    contract = (((0,), (0,)), ((), ()))
    t_up = lax.dot_general(d_cross, low, contract, preferred_element_type=jnp.float32)
    t_down = lax.dot_general(base, d_low, contract, preferred_element_type=jnp.float32)
    t_top = lax.dot_general(mixed, d_pre, contract, preferred_element_type=jnp.float32)
    whole_terms = (jnp.concatenate([t_up, t_down, t_top], axis=1) * scale_factor).reshape(
        n_rep, n_wide, share, grad_cols
    )
    partial_sum = lax.psum_scatter(whole_terms, "wide", scatter_dimension=1, tiled=True)
    summed = summed_on_arrival(partial_sum, "rep", 0).reshape(share, grad_cols)
    bag_rows = d_base.reshape(bags_dev, width)
    outgoing = jnp.where(filled[:, None], bag_rows[bag_pick], jnp.zeros((), jnp.bfloat16))
    hot_in = lax.all_to_all(
        outgoing[: n_wide * capacity].reshape(n_wide, capacity, width),
        "wide",
        split_axis=0,
        concat_axis=0,
        tiled=True,
    )
    cold_part = outgoing[n_wide * capacity :]
    cold_in = lax.all_to_all(
        cold_part.reshape(shards, capacity, width),
        ("rep", "wide"),
        split_axis=0,
        concat_axis=0,
        tiled=True,
    )
    hot_grad = of_everyone(accumulate(hot_in, hot_asked, rows_dev, width), "rep")
    cold_grad = accumulate(cold_in, pieces, rows_dev, width)
    return (
        summed[:, :rank_width],
        summed[:, rank_width : 2 * rank_width],
        summed[:, 2 * rank_width :],
        hot_grad,
        cold_grad,
    )


def solution(mesh):
    placed = (
        P("wide", None),
        P(("rep", "wide"), None),
        P(("rep", "wide"), None),
        P(("rep", "wide"), None),
        P(("rep", "wide")),
        P(),
        P(),
        P(),
        P(),
        P(("rep", "wide"), None),
    )
    return jax.shard_map(
        body,
        mesh=mesh,
        in_specs=placed,
        out_specs=(
            P(("rep", "wide"), None),
            P(("rep", "wide"), None),
            P(("rep", "wide"), None),
            P("wide", None),
            P(("rep", "wide"), None),
        ),
        check_vma=False,
    )
```

profile of v0, /device:TPU:14, one launch (start us, length us, event | category | flops | bytes accessed | tf_op | source)
XLA Modules:
  0.0 608.9 jit_solution(148779887892164052)
XLA Ops:
  9.3 42.3 %while.56 = (s32[]{:T(128)}, s32[12,512]{1,0:T(8,128)S(1)}, s32[6144,1]{0,1:T(1,128)}, s32[12,512]{1,0:T(8,128)S(1)}, s32[12,512]{1,0:T(8,128)S(1)}) while((s32[]{:T(128)}, s32[12,512]{1,0:T(8,128)S(1)}, s32[6144,1]{0,1:T(1,128)}, s32[12,512]{1,0:T(8,128)S(1)}, s32[12,512]{1,0:T(8,128)S(1)}) %tuple.97), condition=%wide.region_2.3_spmd.clone.clone, body=%wide.region_0.2_spmd.clone.sunk.clone | while | flops 15728130 | bytes 43077 | solution.py:37
  52.5 104.6 %while.55 = (s32[]{:T(128)}, s32[20,512]{1,0:T(8,128)S(1)}, s32[20,512]{1,0:T(8,128)S(1)}, s32[20,512]{1,0:T(8,128)S(1)}, s32[6144]{0:T(1024)S(1)}, /*index=5*/s...) while((s32[]{:T(128)}, s32[20,512]{1,0:T(8,128)S(1)}, s32[20,512]{1,0:T(8,128)S(1)}, ...), condition=%wide.region_7.8_spmd.clone, body=%wide.region_3.7_spmd.sunk.clone | while | flops 22018560 | bytes 98405 | solution.py:35
  57.8 5.0 fusion.73
  73.4 5.0 fusion.73
  89.1 5.0 fusion.73
  99.6 5.0 fusion.73
  104.8 5.0 fusion.73
  115.3 5.0 fusion.73
  131.0 5.0 fusion.73
  157.8 8.5 %all-to-all-start = ((s32[32,1,64]{2,1,0:T(1,128)}), s32[32,1,64]{2,1,0:T(1,128)S(1)}, u32[]{:S(2)}, u32[]{:S(2)}) async-start(s32[32,1,64]{2,1,0:T(1,128)} %all_to_all.38), calls=%async_computation | async-start | bytes 32768 | tf_op jit(solution)/shard_map/all_to_all | solution.py:117
  171.7 7.3 %all-to-all-start.2 = ((s32[128,1,64]{2,1,0:T(1,128)}), s32[128,1,64]{2,1,0:T(1,128)S(1)}, u32[]{:S(2)}, u32[]{:S(2)}) async-start(s32[128,1,64]{2,1,0:T(1,128)} %bitcast.10), calls=%async_computation.2 | async-start | bytes 131072 | tf_op jit(solution)/shard_map/all_to_all | solution.py:121
  179.1 8.1 %gather_fusion = bf16[2048,128]{1,0:T(8,128)(2,1)} fusion(bf16[2048,128]{1,0:T(8,128)(2,1)S(1)} %copy-done.6, s32[2048]{0:T(1024)S(1)} %broadcast_clamp_fusion.3), kind=kCustom, calls=%fused_computation | custom fusion | bytes 1056768 | tf_op jit(solution)/shard_map/jit(_take)/gather | solution.py:118
  189.4 7.9 %all-to-all-start.1 = ((bf16[32,64,128]{2,1,0:T(8,128)(2,1)}), bf16[32,64,128]{2,1,0:T(8,128)(2,1)S(1)}, u32[]{:S(2)}, u32[]{:S(2)}) async-start(bf16[32,64,128]{2,1,0:T(8,128)(2,1)} %broadcast_select_fusion.2), calls=%async_computation.1 | async-start | bytes 1048576 | tf_op jit(solution)/shard_map/all_to_all | solution.py:119
  197.4 29.2 %gather_fusion.1 = bf16[8192,128]{1,0:T(8,128)(2,1)} fusion(bf16[2048,128]{1,0:T(8,128)(2,1)S(1)} %copy-done.2, s32[8192]{0:T(1024)S(1)} %broadcast_clamp_fusion.1), kind=kCustom, calls=%fused_computation.1 | custom fusion | bytes 4227072 | tf_op jit(solution)/shard_map/jit(_take)/gather | solution.py:128
  231.0 9.7 %all-to-all-start.3 = ((bf16[128,64,128]{2,1,0:T(8,128)(2,1)}), bf16[128,64,128]{2,1,0:T(8,128)(2,1)}, u32[]{:S(2)}, u32[]{:S(2)}) async-start(bf16[128,64,128]{2,1,0:T(8,128)(2,1)} %broadcast_select_fusion.1), calls=%async_computation.3 | async-start | bytes 4194304 | tf_op jit(solution)/shard_map/all_to_all | solution.py:129
  241.1 26.5 %all-to-all-done.3 = bf16[128,64,128]{2,1,0:T(8,128)(2,1)} async-done(((bf16[128,64,128]{2,1,0:T(8,128)(2,1)}), bf16[128,64,128]{2,1,0:T(8,128)(2,1)}, u32[]{:S(2)}, u32[]{:S(2)}) %all-to-all-start.3) | async-done | bytes 2097184 | tf_op jit(solution)/shard_map/all_to_all | solution.py:129
  271.8 23.2 %gather_fusion.2 = bf16[6144,128]{1,0:T(8,128)(2,1)} fusion(bf16[10240,128]{1,0:T(8,128)(2,1)} %pad_maximum_fusion, s32[6144]{0:T(1024)S(1)} %broadcast_clamp_fusion.2), kind=kCustom, calls=%fused_computation.2 | custom fusion | bytes 3170304 | tf_op jit(solution)/shard_map/gather | solution.py:131
  295.0 41.2 %while.57 = (s32[]{:T(128)}, bf16[8,512,128]{2,1,0:T(8,128)(2,1)}, s32[8]{0:T(128)S(1)}, s32[1,6144]{1,0:T(1,128)S(1)}, bf16[6144,128]{1,0:T(8,128)(2,1)}) while((s32[]{:T(128)}, bf16[8,512,128]{2,1,0:T(8,128)(2,1)}, s32[8]{0:T(128)S(1)}, s32[1,6144]{1,0:T(1,128)S(1)}, bf16[6144,128]{1,0:T(8,128)(2,1)}) %tuple.112), condition=%wide.region_9.10_spmd.clone.clone, body=%wide.region_8.9_spmd.clone.sunk.clone | while | flops 808452608 | bytes 1864269 | solution.py:140
  355.9 10.4 %maximum_multiply_fusion = f32[4,32,32,1024]{3,2,1,0:T(8,128)} fusion(f32[4,32,32,512]{3,2,1,0:T(8,128)} %bitcast.127, f32[4,32,32,256]{3,2,1,0:T(8,128)S(1)} %fusion.37, f32[4,32,32,256]{3,2,1,0:T(8,128)S(1)} %bitcast.128), kind=kLoop, calls=%fused_computation.34 | loop fusion | flops 12582912 | bytes 33554432 | tf_op jit(solution)/shard_map/mul | solution.py:171
  371.5 36.2 %gather_fusion.3 = bf16[10240,128]{1,0:T(8,128)(2,1)} fusion(bf16[4096,128]{1,0:T(8,128)(2,1)S(1)} %reshape.226, s32[10240]{0:T(1024)S(1)} %broadcast_clamp_fusion), kind=kCustom, calls=%fused_computation.3 | custom fusion | bytes 5283840 | tf_op jit(solution)/shard_map/gather | solution.py:177
  407.7 7.0 %broadcast_select_fusion = bf16[10240,128]{1,0:T(8,128)(2,1)S(1)} fusion(bf16[10240,128]{1,0:T(8,128)(2,1)} %gather_fusion.3, pred[10240]{0:T(1024)(128)(4,1)S(1)} %gt.14), kind=kLoop, calls=%fused_computation.44 | loop fusion | flops 1310720 | bytes 5253120 | tf_op jit(solution)/shard_map/jit(_where)/select_n | solution.py:177
  417.0 7.5 %all-to-all-start.5 = ((bf16[32,64,128]{2,1,0:T(8,128)(2,1)}), bf16[32,64,128]{2,1,0:T(8,128)(2,1)S(1)}, u32[]{:S(2)}, u32[]{:S(2)}) async-start(bf16[32,64,128]{2,1,0:T(8,128)(2,1)} %bitcast.25), calls=%async_computation.5 | async-start | bytes 1048576 | tf_op jit(solution)/shard_map/all_to_all | solution.py:178
  427.6 8.2 %all-to-all-done.5 = bf16[32,64,128]{2,1,0:T(8,128)(2,1)S(1)} async-done(((bf16[32,64,128]{2,1,0:T(8,128)(2,1)}), bf16[32,64,128]{2,1,0:T(8,128)(2,1)S(1)}, u32[]{:S(2)}, u32[]{:S(2)}) %all-to-all-start.5) | async-done | bytes 524320 | tf_op jit(solution)/shard_map/all_to_all | solution.py:178
  435.8 7.7 %all-to-all-start.7 = ((bf16[128,64,128]{2,1,0:T(8,128)(2,1)}), bf16[128,64,128]{2,1,0:T(8,128)(2,1)S(1)}, u32[]{:S(2)}, u32[]{:S(2)}) async-start(bf16[128,64,128]{2,1,0:T(8,128)(2,1)} %bitcast.27), calls=%async_computation.7 | async-start | bytes 4194304 | tf_op jit(solution)/shard_map/all_to_all | solution.py:186
  448.3 30.6 %all-to-all-done.7 = bf16[128,64,128]{2,1,0:T(8,128)(2,1)S(1)} async-done(((bf16[128,64,128]{2,1,0:T(8,128)(2,1)}), bf16[128,64,128]{2,1,0:T(8,128)(2,1)S(1)}, u32[]{:S(2)}, u32[]{:S(2)}) %all-to-all-start.7) | async-done | bytes 2097184 | tf_op jit(solution)/shard_map/all_to_all | solution.py:186
  481.2 7.7 %all-to-all-start.6 = ((f32[4,2048,128]{2,1,0:T(8,128)}), f32[4,2048,128]{2,1,0:T(8,128)}, u32[]{:S(2)}, u32[]{:S(2)}) async-start(f32[4,2048,128]{2,1,0:T(8,128)} %broadcast_in_dim.108), calls=%async_computation.6 | async-start | bytes 8388608 | tf_op jit(solution)/shard_map/all_to_all | solution.py:23
  490.4 79.4 %all-reduce.3.cloned.1.call-done = f32[4,32,32,1024]{3,2,1,0:T(8,128)} async-done(((f32[4,32,32,1024]{3,2,1,0:T(8,128)}), f32[4,32,32,1024]{3,2,1,0:T(8,128)}) %all-reduce.3.cloned.1.call-update) | async-done | bytes 16777232
  572.4 5.1 all-to-all-start.4
  577.5 19.6 %while.58 = (s32[]{:T(128)}, f32[2048,128]{1,0:T(8,128)}, s32[4,2048]{1,0:T(4,128)S(1)}, bf16[4,2048,128]{2,1,0:T(8,128)(2,1)S(1)}) while((s32[]{:T(128)}, f32[2048,128]{1,0:T(8,128)}, s32[4,2048]{1,0:T(4,128)S(1)}, bf16[4,2048,128]{2,1,0:T(8,128)(2,1)S(1)}) %tuple.111), condition=%wide.region_14.15_spmd.clone.clone, body=%wide.region_13.14_spmd.clone.sunk.clone | while | flops 1078460416 | bytes 2646087 | solution.py:60
  581.5 5.2 fusion.78
  586.7 5.2 fusion.78
  591.9 5.2 fusion.78
  (258 shorter events, 222.5 us)
Async XLA Ops:
  7.2 332.6 %copy-start = (bf16[4096,256]{1,0:T(8,128)(2,1)S(1)}, bf16[4096,256]{1,0:T(8,128)(2,1)}, u32[]{:S(2)}) copy-start(bf16[4096,256]{1,0:T(8,128)(2,1)} %param.24) | copy-start | bytes 6291460
  7.2 171.9 %copy-start.6 = (bf16[2048,128]{1,0:T(8,128)(2,1)S(1)}, bf16[2048,128]{1,0:T(8,128)(2,1)}, u32[]{:S(2)}) copy-start(bf16[2048,128]{1,0:T(8,128)(2,1)} %param.18) | copy-start | bytes 1572868
  157.8 13.9 %all-to-all-start = ((s32[32,1,64]{2,1,0:T(1,128)}), s32[32,1,64]{2,1,0:T(1,128)S(1)}, u32[]{:S(2)}, u32[]{:S(2)}) async-start(s32[32,1,64]{2,1,0:T(1,128)} %all_to_all.38), calls=%async_computation | async-start | bytes 32768 | tf_op jit(solution)/shard_map/all_to_all | solution.py:117
  171.7 17.7 %all-to-all-start.2 = ((s32[128,1,64]{2,1,0:T(1,128)}), s32[128,1,64]{2,1,0:T(1,128)S(1)}, u32[]{:S(2)}, u32[]{:S(2)}) async-start(s32[128,1,64]{2,1,0:T(1,128)} %bitcast.10), calls=%async_computation.2 | async-start | bytes 131072 | tf_op jit(solution)/shard_map/all_to_all | solution.py:121
  179.1 18.2 %copy-start.2 = (bf16[2048,128]{1,0:T(8,128)(2,1)S(1)}, bf16[2048,128]{1,0:T(8,128)(2,1)}, u32[]{:S(2)}) copy-start(bf16[2048,128]{1,0:T(8,128)(2,1)} %param.19) | copy-start | bytes 1572868
  189.4 41.7 %all-to-all-start.1 = ((bf16[32,64,128]{2,1,0:T(8,128)(2,1)}), bf16[32,64,128]{2,1,0:T(8,128)(2,1)S(1)}, u32[]{:S(2)}, u32[]{:S(2)}) async-start(bf16[32,64,128]{2,1,0:T(8,128)(2,1)} %broadcast_select_fusion.2), calls=%async_computation.1 | async-start | bytes 1048576 | tf_op jit(solution)/shard_map/all_to_all | solution.py:119
  231.0 36.5 %all-to-all-start.3 = ((bf16[128,64,128]{2,1,0:T(8,128)(2,1)}), bf16[128,64,128]{2,1,0:T(8,128)(2,1)}, u32[]{:S(2)}, u32[]{:S(2)}) async-start(bf16[128,64,128]{2,1,0:T(8,128)(2,1)} %broadcast_select_fusion.1), calls=%async_computation.3 | async-start | bytes 4194304 | tf_op jit(solution)/shard_map/all_to_all | solution.py:129
  240.8 329.1 %all-reduce.3.cloned.1.call-start = ((), (), s32[]{:S(2)}) async-start(), calls=%async_computation.8 | async-start | bytes 33554432
  271.8 23.2 %copy-start.10 = (s32[1,6144]{1,0:T(1,128)S(1)}, s32[1,6144]{1,0:T(1,128)}, u32[]{:S(2)}) copy-start(s32[1,6144]{1,0:T(1,128)} %get-tuple-element.542) | copy-start | bytes 73732
  336.1 3.6 copy-start.13
  339.7 2.2 copy-start.7
  341.9 6.6 %copy-start.3 = (f32[128,4096]{1,0:T(8,128)}, f32[128,4096]{1,0:T(8,128)S(1)}, u32[]{:S(2)}) copy-start(f32[128,4096]{1,0:T(8,128)S(1)} %convolution_add_fusion.1) | copy-start | bytes 6291460
  341.9 1.0 copy-start.11
  344.4 1.3 copy-start.5
  353.7 2.2 copy-start.8
  366.3 1.6 copy-start.4
  414.7 1.5 copy-start.9
  417.0 18.8 %all-to-all-start.5 = ((bf16[32,64,128]{2,1,0:T(8,128)(2,1)}), bf16[32,64,128]{2,1,0:T(8,128)(2,1)S(1)}, u32[]{:S(2)}, u32[]{:S(2)}) async-start(bf16[32,64,128]{2,1,0:T(8,128)(2,1)} %bitcast.25), calls=%async_computation.5 | async-start | bytes 1048576 | tf_op jit(solution)/shard_map/all_to_all | solution.py:178
  435.8 8.5 %copy-start.12 = (bf16[32,64,128]{2,1,0:T(8,128)(2,1)}, bf16[32,64,128]{2,1,0:T(8,128)(2,1)S(1)}, u32[]{:S(2)}) copy-start(bf16[32,64,128]{2,1,0:T(8,128)(2,1)S(1)} %all-to-all-done.5) | copy-start | bytes 1572868
  435.8 43.2 %all-to-all-start.7 = ((bf16[128,64,128]{2,1,0:T(8,128)(2,1)}), bf16[128,64,128]{2,1,0:T(8,128)(2,1)S(1)}, u32[]{:S(2)}, u32[]{:S(2)}) async-start(bf16[128,64,128]{2,1,0:T(8,128)(2,1)} %bitcast.27), calls=%async_computation.7 | async-start | bytes 4194304 | tf_op jit(solution)/shard_map/all_to_all | solution.py:186
  481.2 7.7 %copy-start.14 = (u32[128]{0:T(128)S(1)}, u32[128]{0:T(128)}, u32[]{:S(2)}) copy-start(u32[128]{0:T(128)} %constant.104) | copy-start | bytes 1540
  481.2 91.2 %all-to-all-start.6 = ((f32[4,2048,128]{2,1,0:T(8,128)}), f32[4,2048,128]{2,1,0:T(8,128)}, u32[]{:S(2)}, u32[]{:S(2)}) async-start(f32[4,2048,128]{2,1,0:T(8,128)} %broadcast_in_dim.108), calls=%async_computation.6 | async-start | bytes 8388608 | tf_op jit(solution)/shard_map/all_to_all | solution.py:23
  572.4 28.3 %all-to-all-start.4 = ((f32[4,1,1,32,1024]{4,3,2,1,0:T(8,128)}), f32[4,1,1,32,1024]{4,3,2,1,0:T(8,128)S(1)}, u32[]{:S(2)}, u32[]{:S(2)}) async-start(f32[4,1,1,32,1024]{4,3,2,1,0:T(8,128)} %dynamic-slice_bitcast_fusion), calls=%async_computation.4 | async-start | bytes 1048576 | tf_op jit(solution)/shard_map/all_to_all | solution.py:17
  597.1 4.9 copy-start.1
Sparse Core Ops, SparseCore 0:
  366.5 203.3 all-reduce.2
where the time goes:
time: 612 us; the launch traced here: 609 us
  other arithmetic  182 us (30%)
  waiting for transfers between devices  149 us (24%)
  local copies, waits for them, and re-layouts  129 us (21%)
  matrix products  71.5 us (12%)
  starting transfers between devices  61.5 us (10%)
  between operations  14.5 us (2%)
    reduce_sum x20, other arithmetic, slot_info_block(): bag_pick = jnp.sum(jnp.where(match, bag_list[None, :], 0), axis=1)  99.7 us
    unnamed x2, waiting for transfers between devices  79.5 us
    reduce_sum x12, other arithmetic, rank_block(): return jnp.sum(earlier.astype(jnp.int32), axis=1)  41.1 us
    gather x1, local copies, waits for them, and re-layouts, body(): bag_rows[bag_pick]  36.2 us
    dot_general x8, matrix products, pool_block(): return jnp.dot(selector, look_rows, preferred_element_type=jnp.float32)  31.3 us
    all_to_all x1, waiting for transfers between devices, body(): lax.all_to_all(cold_part.reshape(shards, capacity, width), ('rep', 'wide'...  30.6 us
    gather x1, local copies, waits for them, and re-layouts, body(): found = jnp.take(cold_table, pieces, axis=0, mode='fill', fill_value=0)  29.2 us
    all_to_all x1, waiting for transfers between devices, body(): lax.all_to_all(found, ('rep', 'wide'), split_axis=0, concat_axis=0, tiled...  26.5 us
  transfers between devices with their start and end apart: 9, of which 5 were waited for; matrix products, arithmetic and copies ran while one was open for 21% of the time, Pallas kernels for 0%

commit v1 on v0

v1 whole, which is shorter than its diff:
```python
import functools
import math

import jax
import jax.numpy as jnp
from jax import lax
from jax.experimental import pallas as pl
from jax.experimental.pallas import tpu as pltpu
from jax.sharding import PartitionSpec as P

BF = jnp.bfloat16
F32 = jnp.float32
CAP = 64
LANES = 128


def nt_dot(a, b):
    return lax.dot_general(a, b, (((1,), (1,)), ((), ())), preferred_element_type=F32)


def tn_dot(a, b):
    return lax.dot_general(a, b, (((0,), (0,)), ((), ())), preferred_element_type=F32)


def onehot(mask):
    return jnp.where(mask, 1.0, 0.0).astype(BF)


def index_kernel(dest_ref, row_ref, bag_ref, req_ref, bagp_ref, acc_ref, run_ref):
    blocks, width = dest_ref.shape
    dests = run_ref.shape[0]
    slot_rows = req_ref.shape[0]
    upper = lax.broadcasted_iota(jnp.int32, (width, width), 0) < lax.broadcasted_iota(
        jnp.int32, (width, width), 1
    )
    tri = jnp.concatenate([onehot(upper), jnp.ones((width, LANES), BF)], axis=1)
    dest_iota = lax.broadcasted_iota(jnp.int32, (dests, width), 0)
    row_iota = lax.broadcasted_iota(jnp.int32, (slot_rows, width), 0)
    lane_iota = lax.broadcasted_iota(jnp.int32, (LANES, width), 0)
    run_ref[...] = jnp.zeros_like(run_ref)
    acc_ref[...] = jnp.zeros_like(acc_ref)

    def step(k, carry):
        dest = dest_ref[pl.ds(k, 1), :]
        named = dest_iota == dest
        counts = jnp.dot(onehot(named), tri, preferred_element_type=F32)
        run = run_ref[...]
        earlier = counts[:, :width] + jnp.concatenate([run] * (width // LANES), axis=1)
        run_ref[...] = run + counts[:, width:]
        rank = jnp.sum(jnp.where(named, earlier, 0.0), axis=0, keepdims=True).astype(jnp.int32)
        slot = dest * CAP + rank
        left = onehot(row_iota == (slot >> 7))
        place = lane_iota == (slot & 127)
        row = row_ref[pl.ds(k, 1), :]
        bag = bag_ref[pl.ds(k, 1), :]
        parts = []
        for value in ((row >> 7) + 1, row & 127, (bag >> 7) + 1, bag & 127):
            parts.append(jnp.where(place, value.astype(F32), 0.0).astype(BF))
        acc_ref[...] += nt_dot(left, jnp.concatenate(parts, axis=0))
        return carry

    lax.fori_loop(0, blocks, step, 0)
    acc = acc_ref[...].astype(jnp.int32)
    req_ref[...] = (acc[:, :LANES] - 1) * 128 + acc[:, LANES : 2 * LANES]
    bag = (acc[:, 2 * LANES : 3 * LANES] - 1) * 128 + acc[:, 3 * LANES :]
    bagp_ref[...] = jnp.where(bag < 0, -128, (bag & 31) * 128 + (bag >> 5))


def columns_of(idx_row):
    return jnp.transpose(jnp.broadcast_to(idx_row, (LANES, LANES)))


def gather_rows(idx_row, weights, low):
    groups = weights.shape[1] // LANES
    index = columns_of(idx_row)
    lo, hi = index & (low - 1), index >> (low.bit_length() - 1)
    lane = lax.broadcasted_iota(jnp.int32, (LANES, LANES), 1)
    pick = jnp.concatenate([onehot(lo == lane + LANES * t) for t in range(low // LANES)], axis=1)
    found = jnp.dot(pick, weights, preferred_element_type=F32)
    rows = found[:, :LANES]
    for h in range(1, groups):
        rows = jnp.where(hi == h, found[:, h * LANES : (h + 1) * LANES], rows)
    return rows.astype(BF)


def add_rows(idx, rows_ref, start, count, low, groups):
    tall = lax.broadcasted_iota(jnp.int32, (low, LANES), 0)
    lefts, rights = [], []
    for t in range(count // LANES):
        idx_row = idx[t : t + 1, :]
        lefts.append(onehot(tall == (idx_row & (low - 1))))
        hi = columns_of(idx_row) >> (low.bit_length() - 1)
        rows = rows_ref[pl.ds(start + t * LANES, LANES), :]
        rights.append(
            jnp.concatenate(
                [jnp.where(hi == h, rows, jnp.zeros((), BF)) for h in range(groups)], axis=1
            )
        )
    return jnp.dot(
        jnp.concatenate(lefts, axis=1), jnp.concatenate(rights, axis=0), preferred_element_type=F32
    )


def fold(table_ref, folded_ref):
    low = folded_ref.shape[0]
    for h in range(folded_ref.shape[1] // LANES):
        folded_ref[:, h * LANES : (h + 1) * LANES] = table_ref[h * low : (h + 1) * low, :]


def holder_kernel(idx_ref, table_ref, out_ref, folded_ref):
    fold(table_ref, folded_ref)

    def step(k, carry):
        out_ref[pl.ds(pl.multiple_of(k * LANES, LANES), LANES), :] = gather_rows(
            idx_ref[pl.ds(k, 1), :], folded_ref[...], folded_ref.shape[0]
        )
        return carry

    lax.fori_loop(0, idx_ref.shape[0], step, 0)


def accumulate_kernel(idx_ref, rows_ref, out_ref, acc_ref):
    low = acc_ref.shape[0]
    groups = acc_ref.shape[1] // LANES
    acc_ref[...] = jnp.zeros_like(acc_ref)
    per = 8

    def step(k, carry):
        idx = idx_ref[pl.ds(pl.multiple_of(k * per, per), per), :]
        acc_ref[...] += add_rows(
            idx, rows_ref, pl.multiple_of(k * per * LANES, LANES), per * LANES, low, groups
        )
        return carry

    lax.fori_loop(0, idx_ref.shape[0] // per, step, 0)
    for h in range(groups):
        out_ref[h * low : (h + 1) * low, :] = acc_ref[:, h * LANES : (h + 1) * LANES]


def pool_into(bagp_ref, rows_ref, first, acc_ref):
    per = 8
    low, groups = acc_ref.shape[0], acc_ref.shape[1] // LANES

    def step(k, carry):
        idx = bagp_ref[pl.ds(pl.multiple_of(first + k * per, per), per), :]
        acc_ref[...] += add_rows(
            idx, rows_ref, pl.multiple_of(k * per * LANES, LANES), per * LANES, low, groups
        )
        return carry

    lax.fori_loop(0, rows_ref.shape[0] // (per * LANES), step, 0)


def middle_kernel(
    batch,
    bagp_ref,
    hot_ref,
    cold_ref,
    down_hbm,
    up_hbm,
    bias_ref,
    top_hbm,
    dh_ref,
    out_hot_ref,
    out_cold_ref,
    grads_ref,
    down,
    up,
    top,
    acc_ref,
    base,
    cross,
    mixed,
    d_mixed,
    d_cross,
    d_base,
    sems,
):
    loads = [
        pltpu.make_async_copy(source, target, sems.at[n])
        for n, (source, target) in enumerate(((down_hbm, down), (up_hbm, up), (top_hbm, top)))
    ]
    for load in loads:
        load.start()
    acc_ref[...] = jnp.zeros_like(acc_ref)
    pool_into(bagp_ref, hot_ref, 0, acc_ref)
    pool_into(bagp_ref, cold_ref, hot_ref.shape[0] // LANES, acc_ref)
    for load in loads:
        load.wait()
    low_bags, groups = acc_ref.shape[0], acc_ref.shape[1] // LANES
    samples = base.shape[0]
    each = low_bags // samples
    features = each * groups
    for f in range(features):
        base[:, f * LANES : (f + 1) * LANES] = acc_ref[
            (f % each) * samples : (f % each + 1) * samples,
            (f // each) * LANES : (f // each + 1) * LANES,
        ].astype(BF)
    total = base.shape[1]
    step = 512
    spans = [slice(s, s + step) for s in range(0, total, step)]
    low = jnp.dot(base[...], down[...], preferred_element_type=F32).astype(BF)
    preact = jnp.zeros(dh_ref.shape, F32)
    for span in spans:
        part = nt_dot(low, up[span, :]) + bias_ref[:, span]
        full = base[:, span].astype(F32)
        joined = (full * part + full).astype(BF)
        cross[:, span] = part
        mixed[:, span] = joined
        preact += jnp.dot(joined, top[span, :], preferred_element_type=F32)
    sg = 1.0 / (1.0 + jnp.exp(-preact))
    d_pre = (dh_ref[...].astype(F32) * sg * (1.0 + preact * (1.0 - sg))).astype(BF)
    d_low_sum = jnp.zeros(low.shape, F32)
    for span in spans:
        part = nt_dot(d_pre, top[span, :])
        d_mixed[:, span] = part
        crossed = (part * base[:, span].astype(F32)).astype(BF)
        d_cross[:, span] = crossed
        d_low_sum += jnp.dot(crossed, up[span, :], preferred_element_type=F32)
    d_low = d_low_sum.astype(BF)
    for n, span in enumerate(spans):
        part = (d_mixed[:, span] * (cross[:, span] + 1.0) + nt_dot(d_low, down[span, :])).astype(BF)
        for g in range(step // LANES):
            f = n * (step // LANES) + g
            d_base[
                (f % each) * samples : (f % each + 1) * samples,
                (f // each) * LANES : (f // each + 1) * LANES,
            ] = part[:, g * LANES : (g + 1) * LANES]
    scale = 1.0 / math.sqrt(batch)
    rank = low.shape[1]
    for span in spans:
        grads_ref[span, :rank] = (tn_dot(d_cross[:, span], low) * scale).astype(grads_ref.dtype)
        grads_ref[span, rank : 2 * rank] = (tn_dot(base[:, span], d_low) * scale).astype(
            grads_ref.dtype
        )
        grads_ref[span, 2 * rank :] = (tn_dot(mixed[:, span], d_pre) * scale).astype(
            grads_ref.dtype
        )
    hot_rows = out_hot_ref.shape[0] // LANES

    def send_block(out, first):
        def body(k, carry):
            out[pl.ds(pl.multiple_of(k * LANES, LANES), LANES), :] = gather_rows(
                bagp_ref[pl.ds(first + k, 1), :], d_base[...], low_bags
            )
            return carry

        lax.fori_loop(0, out.shape[0] // LANES, body, 0)

    send_block(out_hot_ref, 0)
    send_block(out_cold_ref, hot_rows)


VM = pl.BlockSpec(memory_space=pltpu.VMEM)
ANY = pl.BlockSpec(memory_space=pl.ANY)
LIMIT = 56 << 20


def params(**more):
    return pltpu.CompilerParams(vmem_limit_bytes=LIMIT, **more)


def index_call(dest, row, bag, dests):
    looks = dest.shape[0]
    slot_rows = dests * CAP // LANES
    shape = (looks // 256, 256)
    return pl.pallas_call(
        index_kernel,
        out_shape=[jax.ShapeDtypeStruct((slot_rows, LANES), jnp.int32)] * 2,
        in_specs=[VM] * 3,
        out_specs=[VM] * 2,
        scratch_shapes=[pltpu.VMEM((slot_rows, 4 * LANES), F32), pltpu.VMEM((dests, LANES), F32)],
        compiler_params=params(),
        name="index",
    )(dest.reshape(shape), row.reshape(shape), bag.reshape(shape))


def holder_call(idx, table):
    return pl.pallas_call(
        holder_kernel,
        out_shape=jax.ShapeDtypeStruct((idx.size, LANES), BF),
        in_specs=[VM] * 2,
        out_specs=VM,
        scratch_shapes=[pltpu.VMEM((512, table.shape[0] // 512 * LANES), BF)],
        compiler_params=params(),
        name="holder",
    )(idx, table)


def accumulate_call(idx, rows, table_rows):
    return pl.pallas_call(
        accumulate_kernel,
        out_shape=jax.ShapeDtypeStruct((table_rows, LANES), F32),
        in_specs=[VM] * 2,
        out_specs=VM,
        scratch_shapes=[pltpu.VMEM((512, table_rows // 512 * LANES), F32)],
        compiler_params=params(),
        name="accumulate",
    )(idx, rows)


def middle_call(bagp, hot, cold, down, up, bias, top, d_hidden, batch, grads_dtype):
    samples = d_hidden.shape[0]
    total, rank = down.shape
    units = top.shape[1]
    low_bags = 1024
    groups = total // LANES * samples // low_bags
    return pl.pallas_call(
        functools.partial(middle_kernel, batch),
        out_shape=[
            jax.ShapeDtypeStruct(hot.shape, BF),
            jax.ShapeDtypeStruct(cold.shape, BF),
            jax.ShapeDtypeStruct((total, 2 * rank + units), grads_dtype),
        ],
        in_specs=[VM, VM, VM, ANY, ANY, VM, ANY, VM],
        out_specs=[VM] * 3,
        scratch_shapes=[
            pltpu.VMEM((total, rank), BF),
            pltpu.VMEM((total, rank), BF),
            pltpu.VMEM((total, units), BF),
            pltpu.VMEM((low_bags, groups * LANES), F32),
            pltpu.VMEM((samples, total), BF),
            pltpu.VMEM((samples, total), F32),
            pltpu.VMEM((samples, total), BF),
            pltpu.VMEM((samples, total), F32),
            pltpu.VMEM((samples, total), BF),
            pltpu.VMEM((low_bags, groups * LANES), BF),
            pltpu.SemaphoreType.DMA((3,)),
        ],
        compiler_params=params(),
        name="middle",
    )(bagp, hot, cold, down, up, bias.reshape(1, total), top, d_hidden)


def exchange(value, axes):
    return lax.all_to_all(value, axes, split_axis=0, concat_axis=0, tiled=True)


def body(
    hot_table,
    cold_table,
    bag_of,
    owner,
    row_in,
    cross_down,
    cross_up,
    cross_bias,
    top_weight,
    d_hidden,
):
    n_rep = lax.axis_size("rep")
    n_wide = lax.axis_size("wide")
    shards = n_rep * n_wide
    both = ("rep", "wide")
    rows_dev, width = hot_table.shape
    feat_width, rank = cross_down.shape
    batch = d_hidden.shape[0] * shards
    req, bagp = index_call(owner[:, 0], row_in, bag_of[0], n_wide + shards)
    hot_lanes = n_wide * CAP // LANES
    hot_asked = exchange(req[:hot_lanes].reshape(n_wide, CAP), "wide").reshape(-1, LANES)
    cold_asked = exchange(req[hot_lanes:].reshape(shards, CAP), both).reshape(-1, LANES)
    cold_rows = exchange(holder_call(cold_asked, cold_table).reshape(shards, CAP, width), both)
    hot_rows = exchange(holder_call(hot_asked, hot_table).reshape(n_wide, CAP, width), "wide")
    out_hot, out_cold, terms = middle_call(
        bagp,
        hot_rows.reshape(-1, width),
        cold_rows.reshape(-1, width),
        cross_down,
        cross_up,
        cross_bias,
        top_weight,
        d_hidden,
        batch,
        F32,
    )
    share = feat_width // shards
    partial = lax.psum_scatter(
        terms.reshape(n_rep, n_wide, share, -1), "wide", scatter_dimension=1, tiled=True
    )
    summed = exchange(partial.reshape(n_rep, share, -1), "rep").sum(axis=0)
    cold_in = exchange(out_cold.reshape(shards, CAP, width), both).reshape(-1, width)
    hot_in = exchange(out_hot.reshape(n_wide, CAP, width), "wide").reshape(-1, width)
    hot_part = accumulate_call(hot_asked, hot_in, rows_dev)
    pieces = exchange(hot_part.reshape(n_rep, rows_dev // n_rep, width), "rep").sum(axis=0)
    hot_grad = lax.all_gather(pieces, "rep", tiled=True)
    cold_grad = accumulate_call(cold_asked, cold_in, rows_dev)
    return (
        summed[:, :rank],
        summed[:, rank : 2 * rank],
        summed[:, 2 * rank :],
        hot_grad,
        cold_grad,
    )


def solution(mesh):
    placed = (
        P("wide", None),
        P(("rep", "wide"), None),
        P(("rep", "wide"), None),
        P(("rep", "wide"), None),
        P(("rep", "wide")),
        P(),
        P(),
        P(),
        P(),
        P(("rep", "wide"), None),
    )
    return jax.shard_map(
        body,
        mesh=mesh,
        in_specs=placed,
        out_specs=(
            P(("rep", "wide"), None),
            P(("rep", "wide"), None),
            P(("rep", "wide"), None),
            P("wide", None),
            P(("rep", "wide"), None),
        ),
        check_vma=False,
    )
```

time: 612 us -> 414 us (0.68)
  other arithmetic: 182 us -> 5.17 us
  local copies, waits for them, and re-layouts: 129 us -> 15 us
  Pallas kernels: 0 us -> 110 us
  blocking collectives: 0 us -> 74.6 us
  matrix products: 71.5 us -> 0 us
  starting transfers between devices: 61.5 us -> 35.5 us
  waiting for transfers between devices: 149 us -> 157 us
    reduce_sum x34 -> x2, other arithmetic: 144 us -> 0.79 us  [the longest x1 0.76 us: body(): exchange(hot_part.reshape(n_rep, rows_dev // n_rep, width), 'rep')]
    pallas_call x0 -> x6, Pallas kernels: none -> 110 us  [the longest x1 58.2 us: middle_call(): pl.pallas_call(functools.partial(middle_kernel, batch), out_shape=[jax.Sh...]
    gather x4 -> x0, local copies, waits for them, and re-layouts: 96.6 us -> none  [the longest x1 36.2 us: body(): bag_rows[bag_pick]]
    all_to_all x0 -> x3, blocking collectives: none -> 74.6 us  [exchange(): return lax.all_to_all(value, axes, split_axis=0, concat_axis=0, tiled=True)]
    unnamed x2 -> x3, waiting for transfers between devices: 79.5 us -> 153 us
    dot_general x22 -> x0, matrix products: 71.5 us -> none  [the longest x8 31.3 us: pool_block(): return jnp.dot(selector, look_rows, preferred_element_type=jnp.float32)]
    all_to_all x8 -> x5, waiting for transfers between devices: 69.8 us -> 3.93 us  [exchange(): return lax.all_to_all(value, axes, split_axis=0, concat_axis=0, tiled=True)]
    all_to_all x8 -> x5, starting transfers between devices: 61.3 us -> 35.5 us  [exchange(): return lax.all_to_all(value, axes, split_axis=0, concat_axis=0, tiled=True)]
  transfers between devices with their start and end apart: 9 -> 7, of which waited for: 5 -> 2; matrix products, arithmetic and copies ran while one was open for 21% -> 2% of each run, Pallas kernels for 0% -> 10%
where the time goes in v1:
time: 414 us; the launch traced here: 413 us
  waiting for transfers between devices  157 us (38%)
  Pallas kernels  110 us (27%)
  blocking collectives  74.6 us (18%)
  starting transfers between devices  35.5 us (9%)
  between operations  15.6 us (4%)
  local copies, waits for them, and re-layouts  15 us (4%)
  other arithmetic  5.17 us (1%)
    unnamed x3, waiting for transfers between devices  153 us
    all_to_all x3, blocking collectives, exchange(): return lax.all_to_all(value, axes, split_axis=0, concat_axis=0, tiled=True)  74.6 us
    pallas_call x1, Pallas kernels, middle_call(): pl.pallas_call(functools.partial(middle_kernel, batch), out_shape=[jax.Sh...  58.2 us
    all_to_all x5, starting transfers between devices, exchange(): return lax.all_to_all(value, axes, split_axis=0, concat_axis=0, tiled=True)  35.5 us
    pallas_call x2, Pallas kernels, holder_call(): pl.pallas_call(holder_kernel, out_shape=jax.ShapeDtypeStruct((idx.size, L...  26.7 us
    pallas_call x2, Pallas kernels, accumulate_call(): pl.pallas_call(accumulate_kernel, out_shape=jax.ShapeDtypeStruct((table_r...  13.7 us
    pallas_call x1, Pallas kernels, index_call(): pl.pallas_call(index_kernel, out_shape=[jax.ShapeDtypeStruct((slot_rows,...  11.5 us
  transfers between devices with their start and end apart: 7, of which 2 were waited for; matrix products, arithmetic and copies ran while one was open for 2% of the time, Pallas kernels for 10%

profile of v1, /device:TPU:14, one launch (start us, length us, event | category | flops | bytes accessed | tf_op | source)
XLA Modules:
  0.0 412.9 jit_solution(7969712468207237767)
XLA Ops:
  8.5 1.4 reduce.12
  10.6 1.4 reduce.13
  12.6 1.4 reshape.65.row_ref
  14.0 11.5 %index.1 = (s32[80,128]{1,0:T(8,128)}, s32[80,128]{1,0:T(8,128)}) custom-call(s32[24,256]{1,0:T(8,128)} %reshape_squeeze.6.dest_ref, s32[24,256]{1,0:T(8,128)} %reshape.65.row_ref, s32[24,256]{1,0:T(8,128)} %reshape_squeeze.7.bag_ref), custom_call_target="tpu_custom_call" | custom-call | tf_op jit(solution)/shard_map/index/pallas_call | solution.py:267
  25.5 0.7 slice.15
  26.2 0.7 all_to_all.30
  26.9 8.5 %all-to-all-start = ((s32[32,1,64]{2,1,0:T(1,128)}), s32[32,1,64]{2,1,0:T(1,128)S(1)}, u32[]{:S(2)}, u32[]{:S(2)}) async-start(s32[32,1,64]{2,1,0:T(1,128)} %bitcast.6), calls=%async_computation | async-start | bytes 32768 | tf_op jit(solution)/shard_map/all_to_all | solution.py:336
  35.3 0.8 slice.16
  36.1 0.7 all_to_all.33
  36.8 3.9 all-to-all-done
  40.7 7.3 %all-to-all-start.2 = ((s32[128,1,64]{2,1,0:T(1,128)}), s32[128,1,64]{2,1,0:T(1,128)S(1)}, u32[]{:S(2)}, u32[]{:S(2)}) async-start(s32[128,1,64]{2,1,0:T(1,128)} %bitcast.9), calls=%async_computation.2 | async-start | bytes 131072 | tf_op jit(solution)/shard_map/all_to_all | solution.py:336
  48.0 0.7 reduce.14
  48.7 0.7 reshape.66.idx_ref
  49.4 6.4 %holder.2 = bf16[2048,128]{1,0:T(8,128)(2,1)} custom-call(s32[16,128]{1,0:T(8,128)} %reshape.66.idx_ref, bf16[2048,128]{1,0:T(8,128)(2,1)} %table_ref.2), custom_call_target="tpu_custom_call" | custom-call | tf_op jit(solution)/shard_map/holder/pallas_call | solution.py:279
  55.8 7.9 %all-to-all-start.1 = ((bf16[32,64,128]{2,1,0:T(8,128)(2,1)}), bf16[32,64,128]{2,1,0:T(8,128)(2,1)S(1)}, u32[]{:S(2)}, u32[]{:S(2)}) async-start(bf16[32,64,128]{2,1,0:T(8,128)(2,1)} %bitcast.31), calls=%async_computation.1 | async-start | bytes 1048576 | tf_op jit(solution)/shard_map/all_to_all | solution.py:336
  63.7 0.8 reduce.15
  64.5 0.7 reshape.69.idx_ref
  65.2 20.3 %holder.3 = bf16[8192,128]{1,0:T(8,128)(2,1)} custom-call(s32[64,128]{1,0:T(8,128)} %reshape.69.idx_ref, bf16[2048,128]{1,0:T(8,128)(2,1)} %table_ref.3), custom_call_target="tpu_custom_call" | custom-call | tf_op jit(solution)/shard_map/holder/pallas_call | solution.py:279
  85.5 36.5 %all_to_all.48 = bf16[128,64,128]{2,1,0:T(8,128)(2,1)} all-to-all(bf16[128,64,128]{2,1,0:T(8,128)(2,1)} %bitcast.26), channel_id=1, replica_groups=mesh['rep'=4,'wide'=32] {'rep','wide'}, dimensions={0} | all-to-all | bytes 4194304 | tf_op jit(solution)/shard_map/all_to_all | solution.py:336
  122.0 58.2 %middle.1 = (bf16[2048,128]{1,0:T(8,128)(2,1)}, bf16[8192,128]{1,0:T(8,128)(2,1)}, f32[4096,1024]{1,0:T(8,128)}) custom-call(s32[80,128]{1,0:T(8,128)} %get-tuple-element.10.bagp_ref, bf16[2048,128]{1,0:T(8,128)(2,1)} %bitcast.28, bf16[8192,128]{1,0:T(8,128)(2,1)} %bitcast.24, bf16[4096,256]{1,0:T(8,128)(2,1)} %down_hbm.1, bf16[4096,256]{1,0:T(8,128)(2,1)} %up_hbm.1, ...), custom_call_target="tpu_custom_call" | custom-call | tf_op jit(solution)/shard_map/middle/pallas_call | solution.py:308
  180.2 1.0 copy-done.2
  181.2 18.8 %all_to_all.49 = bf16[32,64,128]{2,1,0:T(8,128)(2,1)} all-to-all(bf16[32,64,128]{2,1,0:T(8,128)(2,1)S(1)} %bitcast.32), channel_id=1, replica_groups=mesh['rep'=4,'wide'=32] {'wide'}, dimensions={0} | all-to-all | bytes 1048576 | tf_op jit(solution)/shard_map/all_to_all | solution.py:336
  200.0 3.9 accumulate.2
  204.0 19.3 %all_to_all.50 = f32[4,512,128]{2,1,0:T(8,128)S(1)} all-to-all(f32[4,512,128]{2,1,0:T(8,128)} %bitcast.27), channel_id=1, replica_groups=mesh['rep'=4,'wide'=32] {'rep'}, dimensions={0} | all-to-all | bytes 2097152 | tf_op jit(solution)/shard_map/all_to_all | solution.py:336
  223.3 7.0 %all-to-all-start.7 = ((bf16[128,64,128]{2,1,0:T(8,128)(2,1)}), bf16[128,64,128]{2,1,0:T(8,128)(2,1)S(1)}, u32[]{:S(2)}, u32[]{:S(2)}) async-start(bf16[128,64,128]{2,1,0:T(8,128)(2,1)} %bitcast.30), calls=%async_computation.7 | async-start | bytes 4194304 | tf_op jit(solution)/shard_map/all_to_all | solution.py:336
  230.4 0.8 reduce_sum.19
  231.8 153.0 %all-reduce.3.cloned.1.call-done = f32[4,32,32,1024]{3,2,1,0:T(8,128)} async-done(((f32[4,32,32,1024]{3,2,1,0:T(8,128)}), f32[4,32,32,1024]{3,2,1,0:T(8,128)}) %all-reduce.3.cloned.1.call-update) | async-done | bytes 16777232
  384.8 2.5 dynamic-slice_bitcast_fusion
  387.3 4.8 %all-to-all-start.4 = ((f32[4,32,1024]{2,1,0:T(8,128)}), f32[4,32,1024]{2,1,0:T(8,128)S(1)}, u32[]{:S(2)}, u32[]{:S(2)}) async-start(f32[4,32,1024]{2,1,0:T(8,128)} %dynamic-slice_bitcast_fusion), calls=%async_computation.4 | async-start | bytes 1048576 | tf_op jit(solution)/shard_map/all_to_all | solution.py:336
  392.2 9.7 %accumulate.3 = f32[2048,128]{1,0:T(8,128)} custom-call(s32[64,128]{1,0:T(8,128)} %reshape.69.idx_ref, bf16[8192,128]{1,0:T(8,128)(2,1)} %bitcast.25), custom_call_target="tpu_custom_call" | custom-call | tf_op jit(solution)/shard_map/accumulate/pallas_call | solution.py:291
  402.5 0.6 slice.22
  403.2 2.3 copy.21
  (22 shorter events, 3.1 us)
Async XLA Ops:
  26.9 13.9 %all-to-all-start = ((s32[32,1,64]{2,1,0:T(1,128)}), s32[32,1,64]{2,1,0:T(1,128)S(1)}, u32[]{:S(2)}, u32[]{:S(2)}) async-start(s32[32,1,64]{2,1,0:T(1,128)} %bitcast.6), calls=%async_computation | async-start | bytes 32768 | tf_op jit(solution)/shard_map/all_to_all | solution.py:336
  40.7 15.0 %all-to-all-start.2 = ((s32[128,1,64]{2,1,0:T(1,128)}), s32[128,1,64]{2,1,0:T(1,128)S(1)}, u32[]{:S(2)}, u32[]{:S(2)}) async-start(s32[128,1,64]{2,1,0:T(1,128)} %bitcast.9), calls=%async_computation.2 | async-start | bytes 131072 | tf_op jit(solution)/shard_map/all_to_all | solution.py:336
  55.8 29.7 %all-to-all-start.1 = ((bf16[32,64,128]{2,1,0:T(8,128)(2,1)}), bf16[32,64,128]{2,1,0:T(8,128)(2,1)S(1)}, u32[]{:S(2)}, u32[]{:S(2)}) async-start(bf16[32,64,128]{2,1,0:T(8,128)(2,1)} %bitcast.31), calls=%async_computation.1 | async-start | bytes 1048576 | tf_op jit(solution)/shard_map/all_to_all | solution.py:336
  63.7 321.1 %all-reduce.3.cloned.1.call-start = ((), (), s32[]{:S(2)}) async-start(), calls=%async_computation.9 | async-start | bytes 33554432
  85.5 36.5 %copy-start.1 = (bf16[32,64,128]{2,1,0:T(8,128)(2,1)}, bf16[32,64,128]{2,1,0:T(8,128)(2,1)S(1)}, u32[]{:S(2)}) copy-start(bf16[32,64,128]{2,1,0:T(8,128)(2,1)S(1)} %all-to-all-done.1) | copy-start | bytes 1572868
  180.2 1.0 copy-start.2
  223.3 7.9 %copy-start.3 = (u32[128]{0:T(128)S(1)}, u32[128]{0:T(128)}, u32[]{:S(2)}) copy-start(u32[128]{0:T(128)} %constant.5) | copy-start | bytes 1540
  223.3 164.0 %all-to-all-start.7 = ((bf16[128,64,128]{2,1,0:T(8,128)(2,1)}), bf16[128,64,128]{2,1,0:T(8,128)(2,1)S(1)}, u32[]{:S(2)}, u32[]{:S(2)}) async-start(bf16[128,64,128]{2,1,0:T(8,128)(2,1)} %bitcast.30), calls=%async_computation.7 | async-start | bytes 4194304 | tf_op jit(solution)/shard_map/all_to_all | solution.py:336
  230.3 171.5 %all-gather.2.cloned.1.call-start = ((), (), s32[]{:S(2)}) async-start(), calls=%async_computation.8 | async-start | bytes 1310720 | tf_op jit(solution)/shard_map/all_gather | solution.py:385
  387.3 4.8 %copy-start = (bf16[128,64,128]{2,1,0:T(8,128)(2,1)}, bf16[128,64,128]{2,1,0:T(8,128)(2,1)S(1)}, u32[]{:S(2)}) copy-start(bf16[128,64,128]{2,1,0:T(8,128)(2,1)S(1)} %all-to-all-done.7) | copy-start | bytes 6291460
  387.3 14.5 %all-to-all-start.4 = ((f32[4,32,1024]{2,1,0:T(8,128)}), f32[4,32,1024]{2,1,0:T(8,128)S(1)}, u32[]{:S(2)}, u32[]{:S(2)}) async-start(f32[4,32,1024]{2,1,0:T(8,128)} %dynamic-slice_bitcast_fusion), calls=%async_computation.4 | async-start | bytes 1048576 | tf_op jit(solution)/shard_map/all_to_all | solution.py:336
Sparse Core Ops, SparseCore 0:
  180.3 204.4 all-reduce.2
Sparse Core Ops, SparseCore 1:
  232.6 31.7 all-gather.1

commit v2 on v1

v2 whole, which is shorter than its diff:
```python
import functools
import math

import jax
import jax.numpy as jnp
from jax import lax
from jax.experimental import pallas as pl
from jax.experimental.pallas import tpu as pltpu
from jax.sharding import PartitionSpec as P

BF = jnp.bfloat16
F32 = jnp.float32
CAP = 64
LANES = 128


def nt_dot(a, b):
    return lax.dot_general(a, b, (((1,), (1,)), ((), ())), preferred_element_type=F32)


def tn_dot(a, b):
    return lax.dot_general(a, b, (((0,), (0,)), ((), ())), preferred_element_type=F32)


def onehot(mask):
    return jnp.where(mask, 1.0, 0.0).astype(BF)


def index_kernel(dest_ref, row_ref, bag_ref, ask_ref, bagp_ref, acc_ref, run_ref):
    blocks, width = dest_ref.shape
    dests = run_ref.shape[0]
    slot_rows = bagp_ref.shape[0]
    upper = lax.broadcasted_iota(jnp.int32, (width, width), 0) < lax.broadcasted_iota(
        jnp.int32, (width, width), 1
    )
    tri = jnp.concatenate([onehot(upper), jnp.ones((width, LANES), BF)], axis=1)
    dest_iota = lax.broadcasted_iota(jnp.int32, (dests, width), 0)
    row_iota = lax.broadcasted_iota(jnp.int32, (slot_rows, width), 0)
    lane_iota = lax.broadcasted_iota(jnp.int32, (LANES, width), 0)
    run_ref[...] = jnp.zeros_like(run_ref)
    acc_ref[...] = jnp.zeros_like(acc_ref)

    per = 4

    def step(k, carry):
        run = run_ref[...]
        total = acc_ref[...]
        for t in range(per):
            at = pl.ds(k * per + t, 1)
            dest = dest_ref[at, :]
            named = dest_iota == dest
            counts = jnp.dot(onehot(named), tri, preferred_element_type=F32)
            earlier = counts[:, :width] + jnp.concatenate([run] * (width // LANES), axis=1)
            run = run + counts[:, width:]
            rank = jnp.sum(jnp.where(named, earlier, 0.0), axis=0, keepdims=True).astype(jnp.int32)
            slot = dest * CAP + rank
            left = onehot(row_iota == (slot >> 7))
            place = lane_iota == (slot & 127)
            row = row_ref[at, :]
            bag = bag_ref[at, :]
            parts = []
            for value in ((row >> 7) + 1, row & 127, (bag >> 7) + 1, bag & 127):
                parts.append(jnp.where(place, value.astype(F32), 0.0).astype(BF))
            total = total + nt_dot(left, jnp.concatenate(parts, axis=0))
        run_ref[...] = run
        acc_ref[...] = total
        return carry

    lax.fori_loop(0, blocks // per, step, 0)
    acc = acc_ref[...].astype(jnp.int32)
    req = (acc[:, :LANES] - 1) * 128 + acc[:, LANES : 2 * LANES]
    half = ask_ref.shape[0] // 2
    cold = req[slot_rows - half :, :]
    hot = jnp.concatenate([req[: slot_rows - half, :]] * (half // (slot_rows - half)), axis=0)
    first = lax.broadcasted_iota(jnp.int32, cold.shape, 1) < CAP
    ask_ref[pl.ds(0, half, stride=2), :] = jnp.where(first, cold, pltpu.roll(hot, CAP, 1))
    ask_ref[pl.ds(1, half, stride=2), :] = jnp.where(first, pltpu.roll(cold, CAP, 1), hot)
    bag = (acc[:, 2 * LANES : 3 * LANES] - 1) * 128 + acc[:, 3 * LANES :]
    bagp_ref[...] = jnp.where(bag < 0, -128, (bag & 31) * 128 + (bag >> 5))


def columns_of(idx_row):
    return jnp.transpose(jnp.broadcast_to(idx_row, (LANES, LANES)))


def gather_rows(idx, weights, low):
    groups = weights.shape[1] // LANES
    shift = low.bit_length() - 1
    lane = lax.broadcasted_iota(jnp.int32, (LANES, LANES), 1)
    picks, his = [], []
    for t in range(idx.shape[0]):
        index = columns_of(idx[t : t + 1, :])
        lo = index & (low - 1)
        his.append(index >> shift)
        picks.append(
            jnp.concatenate([onehot(lo == lane + LANES * u) for u in range(low // LANES)], axis=1)
        )
    found = jnp.dot(jnp.concatenate(picks, axis=0), weights, preferred_element_type=F32)
    hi = jnp.concatenate(his, axis=0)
    rows = found[:, :LANES]
    for h in range(1, groups):
        rows = jnp.where(hi == h, found[:, h * LANES : (h + 1) * LANES], rows)
    return rows.astype(BF)


def gather_all(idx_ref, first, weights_ref, out_ref, per):
    size = per * LANES

    def step(k, carry):
        idx = idx_ref[pl.ds(pl.multiple_of(first + k * per, per), per), :]
        out_ref[pl.ds(pl.multiple_of(k * size, size), size), :] = gather_rows(
            idx, weights_ref[...], weights_ref.shape[0]
        )
        return carry

    lax.fori_loop(0, out_ref.shape[0] // size, step, 0)


def add_rows(idx, rows_ref, start, count, low, groups):
    tall = lax.broadcasted_iota(jnp.int32, (low, LANES), 0)
    lefts, rights = [], []
    for t in range(count // LANES):
        idx_row = idx[t : t + 1, :]
        lefts.append(onehot(tall == (idx_row & (low - 1))))
        hi = columns_of(idx_row) >> (low.bit_length() - 1)
        rows = rows_ref[pl.ds(start + t * LANES, LANES), :]
        rights.append(
            jnp.concatenate(
                [jnp.where(hi == h, rows, jnp.zeros((), BF)) for h in range(groups)], axis=1
            )
        )
    return jnp.dot(
        jnp.concatenate(lefts, axis=1), jnp.concatenate(rights, axis=0), preferred_element_type=F32
    )


def fold(table_ref, folded_ref):
    low = folded_ref.shape[0]
    for h in range(folded_ref.shape[1] // LANES):
        folded_ref[:, h * LANES : (h + 1) * LANES] = table_ref[h * low : (h + 1) * low, :]


def holder_kernel(
    n_wide, asked_ref, hot_ref, cold_ref, hot_rows, cold_rows, hot_idx, cold_idx, fold_hot, fold_cold
):
    fold(hot_ref, fold_hot)
    fold(cold_ref, fold_cold)
    half = asked_ref.shape[0] // 2
    count = n_wide // 2
    begin = lax.axis_index("rep") * n_wide
    even, odd = asked_ref[pl.ds(0, half, stride=2), :], asked_ref[pl.ds(1, half, stride=2), :]
    first = lax.broadcasted_iota(jnp.int32, even.shape, 1) < CAP
    cold_idx[...] = jnp.where(first, even, pltpu.roll(odd, CAP, 1))
    even = asked_ref[pl.ds(begin, count, stride=2), :]
    odd = asked_ref[pl.ds(begin + 1, count, stride=2), :]
    hot_idx[...] = jnp.where(first[:count], pltpu.roll(even, CAP, 1), odd)
    gather_all(cold_idx, 0, fold_cold, cold_rows, 8)
    gather_all(hot_idx, 0, fold_hot, hot_rows, 8)


def accumulate_kernel(idx_ref, rows_ref, out_ref, acc_ref):
    low = acc_ref.shape[0]
    groups = acc_ref.shape[1] // LANES
    acc_ref[...] = jnp.zeros_like(acc_ref)
    per = 8

    def step(k, carry):
        idx = idx_ref[pl.ds(pl.multiple_of(k * per, per), per), :]
        acc_ref[...] += add_rows(
            idx, rows_ref, pl.multiple_of(k * per * LANES, LANES), per * LANES, low, groups
        )
        return carry

    lax.fori_loop(0, idx_ref.shape[0] // per, step, 0)
    for h in range(groups):
        out_ref[h * low : (h + 1) * low, :] = acc_ref[:, h * LANES : (h + 1) * LANES]


def pool_into(bagp_ref, rows_ref, first, acc_ref):
    per = 8
    low, groups = acc_ref.shape[0], acc_ref.shape[1] // LANES

    def step(k, carry):
        idx = bagp_ref[pl.ds(pl.multiple_of(first + k * per, per), per), :]
        acc_ref[...] += add_rows(
            idx, rows_ref, pl.multiple_of(k * per * LANES, LANES), per * LANES, low, groups
        )
        return carry

    lax.fori_loop(0, rows_ref.shape[0] // (per * LANES), step, 0)


def pool_kernel(bagp_ref, hot_ref, cold_ref, base_ref, acc_ref):
    acc_ref[...] = jnp.zeros_like(acc_ref)
    pool_into(bagp_ref, hot_ref, 0, acc_ref)
    pool_into(bagp_ref, cold_ref, hot_ref.shape[0] // LANES, acc_ref)
    samples = base_ref.shape[0]
    each = acc_ref.shape[0] // samples
    for f in range(base_ref.shape[1] // LANES):
        base_ref[:, f * LANES : (f + 1) * LANES] = acc_ref[
            (f % each) * samples : (f % each + 1) * samples,
            (f // each) * LANES : (f // each + 1) * LANES,
        ].astype(BF)


def dense_kernel(
    batch,
    base,
    down,
    up,
    bias_ref,
    top,
    dh_ref,
    d_base,
    grads_ref,
    cross,
    mixed,
    d_mixed,
    d_cross,
):
    samples, total = base.shape
    each = d_base.shape[0] // samples
    step = 512
    spans = [slice(s, s + step) for s in range(0, total, step)]
    low = jnp.dot(base[...], down[...], preferred_element_type=F32).astype(BF)
    preact = jnp.zeros(dh_ref.shape, F32)
    for span in spans:
        part = nt_dot(low, up[span, :]) + bias_ref[:, span]
        full = base[:, span].astype(F32)
        joined = (full * part + full).astype(BF)
        cross[:, span] = part
        mixed[:, span] = joined
        preact += jnp.dot(joined, top[span, :], preferred_element_type=F32)
    sg = 1.0 / (1.0 + jnp.exp(-preact))
    d_pre = (dh_ref[...].astype(F32) * sg * (1.0 + preact * (1.0 - sg))).astype(BF)
    d_low_sum = jnp.zeros(low.shape, F32)
    for span in spans:
        part = nt_dot(d_pre, top[span, :])
        d_mixed[:, span] = part
        crossed = (part * base[:, span].astype(F32)).astype(BF)
        d_cross[:, span] = crossed
        d_low_sum += jnp.dot(crossed, up[span, :], preferred_element_type=F32)
    d_low = d_low_sum.astype(BF)
    for n, span in enumerate(spans):
        part = (d_mixed[:, span] * (cross[:, span] + 1.0) + nt_dot(d_low, down[span, :])).astype(BF)
        for g in range(step // LANES):
            f = n * (step // LANES) + g
            d_base[
                (f % each) * samples : (f % each + 1) * samples,
                (f // each) * LANES : (f // each + 1) * LANES,
            ] = part[:, g * LANES : (g + 1) * LANES]
    scale = 1.0 / math.sqrt(batch)
    rank = low.shape[1]
    for span in spans:
        grads_ref[span, :rank] = (tn_dot(d_cross[:, span], low) * scale).astype(grads_ref.dtype)
        grads_ref[span, rank : 2 * rank] = (tn_dot(base[:, span], d_low) * scale).astype(
            grads_ref.dtype
        )
        grads_ref[span, 2 * rank :] = (tn_dot(mixed[:, span], d_pre) * scale).astype(
            grads_ref.dtype
        )


def send_kernel(bagp_ref, d_base_ref, hot_ref, cold_ref):
    gather_all(bagp_ref, 0, d_base_ref, hot_ref, 4)
    gather_all(bagp_ref, hot_ref.shape[0] // LANES, d_base_ref, cold_ref, 4)


VM = pl.BlockSpec(memory_space=pltpu.VMEM)
ANY = pl.BlockSpec(memory_space=pl.ANY)
LIMIT = 56 << 20


def params(**more):
    return pltpu.CompilerParams(vmem_limit_bytes=LIMIT, **more)


def index_call(dest, row, bag, n_wide, shards):
    looks = dest.shape[0]
    dests = n_wide + shards
    slot_rows = dests * CAP // LANES
    shape = (looks // 256, 256)
    return pl.pallas_call(
        index_kernel,
        out_shape=[
            jax.ShapeDtypeStruct((shards, LANES), jnp.int32),
            jax.ShapeDtypeStruct((slot_rows, LANES), jnp.int32),
        ],
        in_specs=[VM] * 3,
        out_specs=[VM] * 2,
        scratch_shapes=[pltpu.VMEM((slot_rows, 4 * LANES), F32), pltpu.VMEM((dests, LANES), F32)],
        compiler_params=params(),
        name="index",
    )(dest.reshape(shape), row.reshape(shape), bag.reshape(shape))


def holder_call(asked, hot_table, cold_table, n_wide):
    shards = asked.shape[0]
    slots = (n_wide * CAP, shards * CAP)
    return pl.pallas_call(
        functools.partial(holder_kernel, n_wide),
        out_shape=[jax.ShapeDtypeStruct((s, LANES), BF) for s in slots]
        + [jax.ShapeDtypeStruct((s // LANES, LANES), jnp.int32) for s in slots],
        in_specs=[VM] * 3,
        out_specs=[VM] * 4,
        scratch_shapes=[
            pltpu.VMEM((512, table.shape[0] // 512 * LANES), BF) for table in (hot_table, cold_table)
        ],
        compiler_params=params(),
        name="holder",
    )(asked, hot_table, cold_table)


def accumulate_call(idx, rows, table_rows):
    return pl.pallas_call(
        accumulate_kernel,
        out_shape=jax.ShapeDtypeStruct((table_rows, LANES), F32),
        in_specs=[VM] * 2,
        out_specs=VM,
        scratch_shapes=[pltpu.VMEM((512, table_rows // 512 * LANES), F32)],
        compiler_params=params(),
        name="accumulate",
    )(idx, rows)


def pool_call(bagp, hot, cold, samples):
    low_bags = 1024
    bags_groups = 4
    total = low_bags * bags_groups // samples * LANES
    return pl.pallas_call(
        pool_kernel,
        out_shape=jax.ShapeDtypeStruct((samples, total), BF),
        in_specs=[VM] * 3,
        out_specs=VM,
        scratch_shapes=[pltpu.VMEM((low_bags, bags_groups * LANES), F32)],
        compiler_params=params(),
        name="pool",
    )(bagp, hot, cold)


def dense_call(base, down, up, bias, top, d_hidden, batch, grads_dtype):
    samples, total = base.shape
    rank, units = down.shape[1], top.shape[1]
    low_bags = 1024
    groups = total // LANES * samples // low_bags
    return pl.pallas_call(
        functools.partial(dense_kernel, batch),
        out_shape=[
            jax.ShapeDtypeStruct((low_bags, groups * LANES), BF),
            jax.ShapeDtypeStruct((total, 2 * rank + units), grads_dtype),
        ],
        in_specs=[VM] * 6,
        out_specs=[VM] * 2,
        scratch_shapes=[
            pltpu.VMEM((samples, total), F32),
            pltpu.VMEM((samples, total), BF),
            pltpu.VMEM((samples, total), F32),
            pltpu.VMEM((samples, total), BF),
        ],
        compiler_params=params(),
        name="dense",
    )(base, down, up, bias.reshape(1, total), top, d_hidden)


def send_call(bagp, d_base, hot_slots):
    return pl.pallas_call(
        send_kernel,
        out_shape=[
            jax.ShapeDtypeStruct((hot_slots, LANES), BF),
            jax.ShapeDtypeStruct((bagp.size - hot_slots, LANES), BF),
        ],
        in_specs=[VM] * 2,
        out_specs=[VM] * 2,
        compiler_params=params(),
        name="send",
    )(bagp, d_base)


MESH = pl.DeviceIdType.MESH


def place():
    y, wide = lax.axis_index("rep"), lax.axis_index("wide")
    return y, wide // 8, (wide // 2) % 4, wide % 2


def sum_kernel(streams, t_ref, out_ref, core_in, first, in1, second, in2, third, in3, sends, recvs):
    y, x, z, c = place()
    here = (y, x, z)
    barrier = pltpu.get_barrier_semaphore()

    def device(pos, core):
        return (pos[0], pos[1] * 8 + pos[2] * 2 + core)

    def moved(axis, by):
        return tuple((p + by) % 4 if n == axis else p for n, p in enumerate(here))

    partners = [device(here, 1 - c)]
    partners += [device(moved(axis, by), c) for axis in range(3) for by in (1, 2, 3)]
    for partner in partners:
        pl.semaphore_signal(barrier, inc=1, device_id=partner, device_id_type=MESH)
    pl.semaphore_wait(barrier, len(partners))

    def send(n, source, target, partner):
        copy = pltpu.make_async_remote_copy(
            src_ref=source,
            dst_ref=target,
            send_sem=sends.at[n],
            recv_sem=recvs.at[n],
            device_id=partner,
            device_id_type=MESH,
        )
        copy.start()
        return copy

    started = []
    waiting = []
    for n, (cols, order) in enumerate(streams):
        waiting.append(
            send(n, t_ref.at[:, :, :, 1 - c, :, cols], core_in.at[:, :, :, :, cols], device(here, 1 - c))
        )
    started += waiting
    number = len(streams)

    def fan(source, target, cols, axis, rank):
        nonlocal number
        copies = []
        for by in (2, 1, 3):
            to = moved(axis, by)
            index = tuple(to[axis] if d == rank else slice(None) for d in range(rank + 1))
            copies.append(
                send(number, source.at[(*index, Ellipsis, cols)], target.at[by - 1, ..., cols], device(to, c))
            )
            number += 1
        return copies

    rests = [[a for a in range(3)] for _ in streams]
    stage = []
    for n, (cols, order) in enumerate(streams):
        waiting[n].wait_recv()

        def add(i, carry):
            at = (i // 16, (i // 4) % 4, i % 4)
            own = t_ref[(*at, c, slice(None), cols)].astype(F32)
            first[(*at, slice(None), cols)] = (
                own + core_in[(*at, slice(None), cols)].astype(F32)
            ).astype(BF)
            return carry

        lax.fori_loop(0, 64, add, 0)
        rank = rests[n].index(order[0])
        stage.append(fan(first, in1, cols, order[0], rank))
    started += sum(stage, [])
    after = []
    for n, (cols, order) in enumerate(streams):
        for copy in stage[n]:
            copy.wait_recv()
        rank = rests[n].index(order[0])

        def add(i, carry):
            at = [i // 4, i % 4]
            own = list(at)
            own.insert(rank, here[order[0]])
            total = first[(*own, slice(None), cols)].astype(F32)
            for k in range(3):
                total += in1[(k, *at, slice(None), cols)].astype(F32)
            second[(*at, slice(None), cols)] = total.astype(BF)
            return carry

        lax.fori_loop(0, 16, add, 0)
        rests[n].remove(order[0])
        after.append(fan(second, in2, cols, order[1], rests[n].index(order[1])))
    started += sum(after, [])
    last = []
    for n, (cols, order) in enumerate(streams):
        for copy in after[n]:
            copy.wait_recv()
        rank = rests[n].index(order[1])

        def add(i, carry):
            own = [i]
            own.insert(rank, here[order[1]])
            total = second[(*own, slice(None), cols)].astype(F32)
            for k in range(3):
                total += in2[(k, i, slice(None), cols)].astype(F32)
            third[i, :, cols] = total
            return carry

        lax.fori_loop(0, 4, add, 0)
        rests[n].remove(order[1])
        last.append(fan(third, in3, cols, order[2], 0))
    started += sum(last, [])
    for n, (cols, order) in enumerate(streams):
        for copy in last[n]:
            copy.wait_recv()
        total = third[here[order[2]], :, cols]
        for k in range(3):
            total += in3[k, :, cols]
        out_ref[:, cols] = total
    for copy in started:
        copy.wait_send()


def sum_call(terms, share):
    columns = terms.shape[1]
    step = columns // 8 // LANES * LANES
    cuts = [0, 3 * step, 6 * step, columns]
    orders = ((0, 1, 2), (1, 2, 0), (2, 0, 1))
    streams = [(slice(cuts[n], cuts[n + 1]), orders[n]) for n in range(3)]
    copies = 3 + 27
    return pl.pallas_call(
        functools.partial(sum_kernel, streams),
        out_shape=jax.ShapeDtypeStruct((share, columns), F32),
        in_specs=[VM],
        out_specs=VM,
        scratch_shapes=[
            pltpu.VMEM((4, 4, 4, share, columns), BF),
            pltpu.VMEM((4, 4, 4, share, columns), BF),
            pltpu.VMEM((3, 4, 4, share, columns), BF),
            pltpu.VMEM((4, 4, share, columns), BF),
            pltpu.VMEM((3, 4, share, columns), BF),
            pltpu.VMEM((4, share, columns), F32),
            pltpu.VMEM((3, share, columns), F32),
            pltpu.SemaphoreType.DMA((copies,)),
            pltpu.SemaphoreType.DMA((copies,)),
        ],
        compiler_params=params(collective_id=1, has_side_effects=True),
        name="dense_sum",
    )(terms.reshape(4, 4, 4, 2, share, columns))


def exchange(value, axes):
    return lax.all_to_all(value, axes, split_axis=0, concat_axis=0, tiled=True)


def body(
    hot_table,
    cold_table,
    bag_of,
    owner,
    row_in,
    cross_down,
    cross_up,
    cross_bias,
    top_weight,
    d_hidden,
):
    n_rep = lax.axis_size("rep")
    n_wide = lax.axis_size("wide")
    shards = n_rep * n_wide
    both = ("rep", "wide")
    rows_dev, width = hot_table.shape
    feat_width, rank = cross_down.shape
    batch = d_hidden.shape[0] * shards
    ask, bagp = index_call(owner[:, 0], row_in, bag_of[0], n_wide, shards)
    asked = exchange(ask[:, None, :], both).reshape(shards, LANES)
    hot_found, cold_found, hot_asked, cold_asked = holder_call(asked, hot_table, cold_table, n_wide)
    hot_rows = exchange(hot_found.reshape(n_wide, CAP, width), "wide").reshape(-1, width)
    cold_rows = exchange(cold_found.reshape(shards, CAP, width), both).reshape(-1, width)
    base = pool_call(bagp, hot_rows, cold_rows, d_hidden.shape[0])
    d_base, terms = dense_call(
        base, cross_down, cross_up, cross_bias, top_weight, d_hidden, batch, BF
    )
    out_hot, out_cold = send_call(bagp, d_base, n_wide * CAP)
    hot_in = exchange(out_hot.reshape(n_wide, CAP, width), "wide").reshape(-1, width)
    cold_in = exchange(out_cold.reshape(shards, CAP, width), both).reshape(-1, width)
    summed = sum_call(terms, feat_width // shards)
    hot_part = accumulate_call(hot_asked, hot_in, rows_dev)
    pieces = exchange(hot_part.reshape(n_rep, rows_dev // n_rep, width), "rep").sum(axis=0)
    hot_grad = lax.all_gather(pieces, "rep", tiled=True)
    cold_grad = accumulate_call(cold_asked, cold_in, rows_dev)
    return (
        summed[:, :rank],
        summed[:, rank : 2 * rank],
        summed[:, 2 * rank :],
        hot_grad,
        cold_grad,
    )


def solution(mesh):
    placed = (
        P("wide", None),
        P(("rep", "wide"), None),
        P(("rep", "wide"), None),
        P(("rep", "wide"), None),
        P(("rep", "wide")),
        P(),
        P(),
        P(),
        P(),
        P(("rep", "wide"), None),
    )
    return jax.shard_map(
        body,
        mesh=mesh,
        in_specs=placed,
        out_specs=(
            P(("rep", "wide"), None),
            P(("rep", "wide"), None),
            P(("rep", "wide"), None),
            P("wide", None),
            P(("rep", "wide"), None),
        ),
        check_vma=False,
    )
```

time: 414 us -> 289 us (0.70)
  waiting for transfers between devices: 157 us -> 0.02 us
  Pallas kernels: 110 us -> 146 us
  blocking collectives: 74.6 us -> 105 us
  starting transfers between devices: 35.5 us -> 7.05 us
  local copies, waits for them, and re-layouts: 15 us -> 9.57 us
    unnamed x3 -> x1, waiting for transfers between devices: 153 us -> 0.02 us
    pallas_call x4 -> x6, Pallas kernels: 96.3 us -> 132 us  [the longest x1 63.9 us: sum_call(): pl.pallas_call(functools.partial(sum_kernel, streams), out_shape=jax.Shap...]
    all_to_all x3 -> x5, blocking collectives: 74.6 us -> 105 us  [exchange(): return lax.all_to_all(value, axes, split_axis=0, concat_axis=0, tiled=True)]
    all_to_all x5 -> x1, starting transfers between devices: 35.5 us -> 7.01 us  [exchange(): return lax.all_to_all(value, axes, split_axis=0, concat_axis=0, tiled=True)]
  transfers between devices with their start and end apart: 7 -> 2, of which waited for: 2 -> 0; matrix products, arithmetic and copies ran while one was open for 2% -> 1% of each run, Pallas kernels for 10% -> 26%
where the time goes in v2:
time: 289 us; the launch traced here: 286 us
  Pallas kernels  146 us (51%)
  blocking collectives  105 us (36%)
  between operations  14.1 us (5%)
  local copies, waits for them, and re-layouts  9.57 us (3%)
  starting transfers between devices  7.05 us (2%)
  other arithmetic  3.65 us (1%)
    all_to_all x5, blocking collectives, exchange(): return lax.all_to_all(value, axes, split_axis=0, concat_axis=0, tiled=True)  105 us
    pallas_call x1, Pallas kernels, sum_call(): pl.pallas_call(functools.partial(sum_kernel, streams), out_shape=jax.Shap...  63.9 us
    pallas_call x1, Pallas kernels, send_call(): pl.pallas_call(send_kernel, out_shape=[jax.ShapeDtypeStruct((hot_slots, L...  17.8 us
    pallas_call x1, Pallas kernels, pool_call(): pl.pallas_call(pool_kernel, out_shape=jax.ShapeDtypeStruct((samples, tota...  16.8 us
    pallas_call x1, Pallas kernels, dense_call(): pl.pallas_call(functools.partial(dense_kernel, batch), out_shape=[jax.Sha...  14.5 us
    pallas_call x2, Pallas kernels, accumulate_call(): pl.pallas_call(accumulate_kernel, out_shape=jax.ShapeDtypeStruct((table_r...  13.6 us
    pallas_call x1, Pallas kernels, holder_call(): pl.pallas_call(functools.partial(holder_kernel, n_wide), out_shape=[jax.S...  10 us
    pallas_call x1, Pallas kernels, index_call(): pl.pallas_call(index_kernel, out_shape=[jax.ShapeDtypeStruct((shards, LAN...  9.24 us
  transfers between devices with their start and end apart: 2, of which 0 were waited for; matrix products, arithmetic and copies ran while one was open for 1% of the time, Pallas kernels for 26%

profile of v2, /device:TPU:14, one launch (start us, length us, event | category | flops | bytes accessed | tf_op | source)
XLA Modules:
  0.0 285.6 jit_solution(4559130785829984886)
XLA Ops:
  7.2 0.5 broadcast.6
  7.7 1.4 reduce.7
  9.1 0.6 reshape_squeeze.7.bag_ref
  9.7 1.4 reduce.6
  11.2 0.6 reshape_squeeze.6.dest_ref
  11.8 1.4 reshape.49.row_ref
  13.1 9.2 %index.1 = (s32[128,128]{1,0:T(8,128)}, s32[80,128]{1,0:T(8,128)}) custom-call(s32[24,256]{1,0:T(8,128)} %reshape_squeeze.6.dest_ref, s32[24,256]{1,0:T(8,128)} %reshape.49.row_ref, s32[24,256]{1,0:T(8,128)} %reshape_squeeze.7.bag_ref), custom_call_target="tpu_custom_call" | custom-call | tf_op jit(solution)/shard_map/index/pallas_call | solution.py:283
  22.4 18.0 %all_to_all.30 = s32[128,1,128]{2,1,0:T(1,128)} all-to-all(s32[128,1,128]{2,1,0:T(1,128)} %bitcast.27), channel_id=1, replica_groups=mesh['rep'=4,'wide'=32] {'rep','wide'}, dimensions={0} | all-to-all | bytes 131072 | tf_op jit(solution)/shard_map/all_to_all | solution.py:533
  40.4 10.0 %holder.1 = (bf16[2048,128]{1,0:T(8,128)(2,1)}, bf16[8192,128]{1,0:T(8,128)(2,1)}, s32[16,128]{1,0:T(8,128)}, s32[64,128]{1,0:T(8,128)}) custom-call(s32[128,128]{1,0:T(8,128)} %bitcast.26, bf16[2048,128]{1,0:T(8,128)(2,1)} %hot_ref.1, bf16[2048,128]{1,0:T(8,128)(2,1)} %cold_ref.1), custom_call_target="tpu_custom_call" | custom-call | tf_op jit(solution)/shard_map/holder/pallas_call | solution.py:300
  50.4 16.1 %all_to_all.31 = bf16[32,64,128]{2,1,0:T(8,128)(2,1)} all-to-all(bf16[32,64,128]{2,1,0:T(8,128)(2,1)} %bitcast.24), channel_id=1, replica_groups=mesh['rep'=4,'wide'=32] {'wide'}, dimensions={0} | all-to-all | bytes 1048576 | tf_op jit(solution)/shard_map/all_to_all | solution.py:533
  66.6 34.5 %all_to_all.32 = bf16[128,64,128]{2,1,0:T(8,128)(2,1)} all-to-all(bf16[128,64,128]{2,1,0:T(8,128)(2,1)} %bitcast.23), channel_id=1, replica_groups=mesh['rep'=4,'wide'=32] {'rep','wide'}, dimensions={0} | all-to-all | bytes 4194304 | tf_op jit(solution)/shard_map/all_to_all | solution.py:533
  101.1 16.8 %pool.1.base = bf16[128,4096]{1,0:T(8,128)(2,1)} custom-call(s32[80,128]{1,0:T(8,128)} %get-tuple-element.15.bagp_ref, bf16[2048,128]{1,0:T(8,128)(2,1)} %bitcast.20, bf16[8192,128]{1,0:T(8,128)(2,1)} %bitcast.16), custom_call_target="tpu_custom_call" | custom-call | tf_op jit(solution)/shard_map/pool/pallas_call | solution.py:330
  117.9 14.5 %dense.1 = (bf16[1024,512]{1,0:T(8,128)(2,1)}, bf16[4096,1024]{1,0:T(8,128)(2,1)}) custom-call(bf16[128,4096]{1,0:T(8,128)(2,1)} %pool.1.base, bf16[4096,256]{1,0:T(8,128)(2,1)} %down.1, bf16[4096,256]{1,0:T(8,128)(2,1)} %up.1, f32[1,4096]{1,0:T(1,128)} %bitcast.28, bf16[4096,512]{1,0:T(8,128)(2,1)} %top.1, bf16[128,512]{1,0:T(8,128)(2,1)} %dh_ref.1), custom_call_target="tpu_custom_call" | custom-call | tf_op jit(solution)/shard_map/dense/pallas_call | solution.py:346
  132.4 17.8 %send.1 = (bf16[2048,128]{1,0:T(8,128)(2,1)}, bf16[8192,128]{1,0:T(8,128)(2,1)}) custom-call(s32[80,128]{1,0:T(8,128)} %get-tuple-element.15.bagp_ref, bf16[1024,512]{1,0:T(8,128)(2,1)} %get-tuple-element.21.d_base_ref), custom_call_target="tpu_custom_call" | custom-call | tf_op jit(solution)/shard_map/send/pallas_call | solution.py:366
  150.2 17.3 %all_to_all.33 = bf16[32,64,128]{2,1,0:T(8,128)(2,1)} all-to-all(bf16[32,64,128]{2,1,0:T(8,128)(2,1)} %bitcast.25), channel_id=1, replica_groups=mesh['rep'=4,'wide'=32] {'wide'}, dimensions={0} | all-to-all | bytes 1048576 | tf_op jit(solution)/shard_map/all_to_all | solution.py:533
  167.4 3.9 %accumulate.2 = f32[2048,128]{1,0:T(8,128)} custom-call(s32[16,128]{1,0:T(8,128)} %get-tuple-element.20.idx_ref, bf16[2048,128]{1,0:T(8,128)(2,1)} %bitcast.21), custom_call_target="tpu_custom_call" | custom-call | tf_op jit(solution)/shard_map/accumulate/pallas_call | solution.py:315
  171.3 19.4 %all_to_all.34 = f32[4,512,128]{2,1,0:T(8,128)S(1)} all-to-all(f32[4,512,128]{2,1,0:T(8,128)} %bitcast.19), channel_id=1, replica_groups=mesh['rep'=4,'wide'=32] {'rep'}, dimensions={0} | all-to-all | bytes 2097152 | tf_op jit(solution)/shard_map/all_to_all | solution.py:533
  190.7 7.0 %all-to-all-start.5 = ((bf16[128,64,128]{2,1,0:T(8,128)(2,1)}), bf16[128,64,128]{2,1,0:T(8,128)(2,1)S(1)}, u32[]{:S(2)}, u32[]{:S(2)}) async-start(bf16[128,64,128]{2,1,0:T(8,128)(2,1)} %bitcast.22), calls=%async_computation.5 | async-start | bytes 4194304 | tf_op jit(solution)/shard_map/all_to_all | solution.py:533
  197.8 0.0 all-gather.2.cloned.1.call-start
  197.8 0.8 reduce_sum.9
  198.6 0.0 all-gather.2.cloned.1.call-update
  198.6 63.9 %dense_sum.1 = f32[32,1024]{1,0:T(8,128)} custom-call(bf16[4,4,4,2,32,1024]{5,4,3,2,1,0:T(8,128)(2,1)} %bitcast.17), custom_call_target="tpu_custom_call" | custom-call | tf_op jit(solution)/shard_map/dense_sum/pallas_call | solution.py:511
  262.5 1.5 slice.11
  264.0 1.4 fusion
  265.4 0.0 all-to-all-done.5
  265.4 0.0 copy-start
  265.4 1.3 copy-done
  266.7 9.7 %accumulate.3 = f32[2048,128]{1,0:T(8,128)} custom-call(s32[64,128]{1,0:T(8,128)} %get-tuple-element.23.idx_ref, bf16[8192,128]{1,0:T(8,128)(2,1)} %bitcast.18), custom_call_target="tpu_custom_call" | custom-call | tf_op jit(solution)/shard_map/accumulate/pallas_call | solution.py:315
  276.5 0.0 all-gather.2.cloned.1.call-done
  276.5 2.3 copy.17
Async XLA Ops:
  190.7 74.7 %all-to-all-start.5 = ((bf16[128,64,128]{2,1,0:T(8,128)(2,1)}), bf16[128,64,128]{2,1,0:T(8,128)(2,1)S(1)}, u32[]{:S(2)}, u32[]{:S(2)}) async-start(bf16[128,64,128]{2,1,0:T(8,128)(2,1)} %bitcast.22), calls=%async_computation.5 | async-start | bytes 4194304 | tf_op jit(solution)/shard_map/all_to_all | solution.py:533
  197.8 78.7 %all-gather.2.cloned.1.call-start = ((), (), s32[]{:S(2)}) async-start(), calls=%async_computation.6 | async-start | bytes 1310720 | tf_op jit(solution)/shard_map/all_gather | solution.py:570
  265.4 1.3 copy-start
Sparse Core Ops, SparseCore 0:
  200.8 46.7 all-gather.1
